TPU v7x, 32 devices: a whole 2x2x4 slice. The times are simulated.
32 devices in a mesh: dp: 16 (over z, y, x), tensor: 2 (over core).
Axes of the slice: x: 2, y: 2, z: 4, core: 2. Of those that a mesh axis runs over, the one named last changes fastest.
Arguments:
- images: bfloat16 [2, 96, 197, 768], P(None, 'dp'), may hold values from -6 to 6
- live_images: int32 [2, 16], P(None, 'dp'), may hold values from 1 to 6, as said below
- ln1_gain: bfloat16 [768], P('dp'), may hold values from 0.5 to 1.5
- ln1_bias: bfloat16 [768], P('dp'), may hold values from -3 to 3
- qkv_weight: bfloat16 [768, 3, 768], P('dp', None, 'tensor'), may hold values from -1 to 1
- qkv_bias: bfloat16 [2, 768], P(None, ('tensor', 'dp')), may hold values from -3 to 3
- proj_weight: bfloat16 [768, 768], P('tensor', 'dp'), may hold values from -0.875 to 0.875
- proj_bias: bfloat16 [768], P('dp'), may hold values from -3 to 3
- ln2_gain: bfloat16 [768], P('dp'), may hold values from 0.5 to 1.5
- ln2_bias: bfloat16 [768], P('dp'), may hold values from -3 to 3
- fc1_weight: bfloat16 [768, 3072], P('dp', 'tensor'), may hold values from -0.21875 to 0.21875
- fc1_bias: bfloat16 [3072], P(('tensor', 'dp')), may hold values from -3 to 3
- fc2_weight: bfloat16 [3072, 768], P('tensor', 'dp'), may hold values from -0.109375 to 0.109375
- fc2_bias: bfloat16 [768], P('dp'), may hold values from -3 to 3
- cotangent: bfloat16 [2, 96, 197, 768], P(None, 'dp'), may hold values from -6 to 6
Outputs:
- activations: bfloat16 [2, 96, 197, 768], P(None, 'dp')
- input_grad: float32 [2, 96, 197, 768], P(None, 'dp')
- grad_ln1_gain: float32 [768], P('dp')
- grad_ln1_bias: float32 [768], P('dp')
- grad_qkv_weight: float32 [768, 3, 768], P('dp', None, 'tensor')
- grad_qkv_bias: float32 [2, 768], P(None, ('tensor', 'dp'))
- grad_proj_weight: float32 [768, 768], P('tensor', 'dp')
- grad_proj_bias: float32 [768], P('dp')
- grad_ln2_gain: float32 [768], P('dp')
- grad_ln2_bias: float32 [768], P('dp')
- grad_fc1_weight: float32 [768, 3072], P('dp', 'tensor')
- grad_fc1_bias: float32 [3072], P(('tensor', 'dp'))
- grad_fc2_weight: float32 [3072, 768], P('tensor', 'dp')
- grad_fc2_bias: float32 [768], P('dp')
Inputs may be any that keep to these rules, and one draw needn't show every extreme that they name: live_images[b, r] is how many of data rank r's 6 slots of micro-batch b hold live images, slots 0 upward; in each micro-batch some rank has all 6 live and some rank one.
All inputs are finite; a program needn't handle non-finite values.
Results may differ from a plain program's by a relative error of at most 0.015.
Values may be sent and summed in bfloat16 or wider, within the bound.
No kernel may reach another device: no remote copies, remote signals or barrier semaphores. Data moves between devices by JAX's collectives and lax.ppermute only.
A program may use at most 256 MiB of HBM per device.

v0:
```python
import jax
import jax.numpy as jnp
from jax import lax
from jax.sharding import PartitionSpec as P

HD = 64


eps = 1e-06


def layer_norm(values, gain, shift):
    center = jnp.mean(values, axis=-1, keepdims=True)
    offset = values - center
    variance = jnp.mean(offset * offset, axis=-1, keepdims=True)
    inverse = lax.rsqrt(variance + eps)
    scaled = offset * inverse
    return (scaled * gain + shift, scaled, inverse)


def norm_back(grad_norm, scaled, inverse, gain):
    weighted = grad_norm * gain
    first_mean = jnp.mean(weighted, axis=-1, keepdims=True)
    second_mean = jnp.mean(weighted * scaled, axis=-1, keepdims=True)
    return inverse * (weighted - first_mean - scaled * second_mean)


def gelu_exact(values):
    return jax.nn.gelu(values, approximate=False)


def inner_rows(operand, factor):
    return lax.dot_general(
        operand, factor, (((0,), (0,)), ((), ())), preferred_element_type=jnp.float32
    )


def outer_cols(operand, factor):
    return lax.dot_general(
        operand, factor, (((1,), (1,)), ((), ())), preferred_element_type=jnp.float32
    )


def per_device(
    images,
    live_images,
    ln1_gain,
    ln1_bias,
    qkv_weight,
    qkv_bias,
    proj_weight,
    proj_bias,
    ln2_gain,
    ln2_bias,
    fc1_weight,
    fc1_bias,
    fc2_weight,
    fc2_bias,
    cotangent,
):
    micro, slots, seq_len, width = images.shape
    row_count = slots * seq_len
    scale = HD ** (-0.5)
    outputs = []
    in_grads = []
    totals = None
    owned = None
    for batch in range(micro):
        gathered = (
            lax.all_gather(ln1_gain, "dp", axis=0, tiled=True),
            lax.all_gather(ln1_bias, "dp", axis=0, tiled=True),
            lax.all_gather(qkv_weight, "dp", axis=0, tiled=True),
            lax.all_gather(qkv_bias, "dp", axis=1, tiled=True),
            lax.all_gather(proj_weight, "dp", axis=1, tiled=True),
            lax.all_gather(proj_bias, "dp", axis=0, tiled=True),
            lax.all_gather(ln2_gain, "dp", axis=0, tiled=True),
            lax.all_gather(ln2_bias, "dp", axis=0, tiled=True),
            lax.all_gather(fc1_weight, "dp", axis=0, tiled=True),
            lax.all_gather(fc1_bias, "dp", axis=0, tiled=True),
            lax.all_gather(fc2_weight, "dp", axis=1, tiled=True),
            lax.all_gather(fc2_bias, "dp", axis=0, tiled=True),
        )
        (
            gain_one,
            shift_one,
            w_qkv,
            b_qkv,
            w_proj,
            b_proj,
            gain_two,
            shift_two,
            w_fc1,
            b_fc1,
            w_fc2,
            b_fc2,
        ) = gathered
        group_cols = w_qkv.shape[2]
        heads_here = group_cols // HD
        alive = (jnp.arange(slots) < live_images[batch, 0]).astype(jnp.float32)
        alive_rows = jnp.broadcast_to(alive[:, None, None], (slots, seq_len, 1)).reshape(
            row_count, 1
        )
        inputs_f = images[batch].astype(jnp.float32).reshape(row_count, width)
        normed_one, scaled_one, inverse_one = layer_norm(
            inputs_f, gain_one.astype(jnp.float32), shift_one.astype(jnp.float32)
        )
        normed_one = normed_one.astype(jnp.bfloat16)
        mixed = jnp.dot(
            normed_one, w_qkv.reshape(width, 3 * group_cols), preferred_element_type=jnp.float32
        )
        bias_full = jnp.stack([b_qkv[0], jnp.zeros_like(b_qkv[0]), b_qkv[1]]).astype(jnp.float32)
        mixed = (mixed.reshape(row_count, 3, group_cols) + bias_full).astype(jnp.bfloat16)
        query = mixed[:, 0].reshape(slots, seq_len, heads_here, HD)
        keys_all = mixed[:, 1].reshape(slots, seq_len, heads_here, HD)
        values_all = mixed[:, 2].reshape(slots, seq_len, heads_here, HD)
        scores = (
            jnp.einsum("gqhe,gkhe->ghqk", query, keys_all, preferred_element_type=jnp.float32)
            * scale
        )
        log_total = jax.nn.logsumexp(scores, axis=-1)
        probs = jnp.exp(scores - log_total[..., None]).astype(jnp.bfloat16)
        context = jnp.einsum(
            "ghqk,gkhe->gqhe", probs, values_all, preferred_element_type=jnp.float32
        )
        context = context.astype(jnp.bfloat16).reshape(row_count, group_cols)
        attn_part = jnp.dot(context, w_proj, preferred_element_type=jnp.float32)
        attn_total = lax.psum(attn_part.astype(jnp.bfloat16), "tensor").astype(jnp.float32)
        resid_one = inputs_f + attn_total + b_proj.astype(jnp.float32)
        normed_two, scaled_two, inverse_two = layer_norm(
            resid_one, gain_two.astype(jnp.float32), shift_two.astype(jnp.float32)
        )
        normed_two = normed_two.astype(jnp.bfloat16)
        before = jnp.dot(normed_two, w_fc1, preferred_element_type=jnp.float32) + b_fc1.astype(
            jnp.float32
        )
        hidden = gelu_exact(before).astype(jnp.bfloat16)
        mlp_part = jnp.dot(hidden, w_fc2, preferred_element_type=jnp.float32)
        mlp_total = lax.psum(mlp_part.astype(jnp.bfloat16), "tensor").astype(jnp.float32)
        result = (resid_one + mlp_total + b_fc2.astype(jnp.float32)) * alive_rows
        outputs.append(result.astype(jnp.bfloat16).reshape(slots, seq_len, width))
        regathered = (
            lax.all_gather(ln1_gain, "dp", axis=0, tiled=True),
            lax.all_gather(qkv_weight, "dp", axis=0, tiled=True),
            lax.all_gather(proj_weight, "dp", axis=1, tiled=True),
            lax.all_gather(ln2_gain, "dp", axis=0, tiled=True),
            lax.all_gather(fc1_weight, "dp", axis=0, tiled=True),
            lax.all_gather(fc2_weight, "dp", axis=1, tiled=True),
        )
        gain_one, w_qkv, w_proj, gain_two, w_fc1, w_fc2 = regathered
        grad_out = cotangent[batch].astype(jnp.float32).reshape(row_count, width) * alive_rows
        grad_out_b = grad_out.astype(jnp.bfloat16)
        delta_fc2_bias = jnp.sum(grad_out, axis=0)
        delta_fc2_weight = inner_rows(hidden, grad_out_b)
        grad_hidden = outer_cols(grad_out_b, w_fc2)
        grad_before = jax.vjp(gelu_exact, before)[1](grad_hidden)[0]
        grad_before_b = grad_before.astype(jnp.bfloat16)
        delta_fc1_bias = jnp.sum(grad_before, axis=0)
        delta_fc1_weight = inner_rows(normed_two, grad_before_b)
        norm_two_part = outer_cols(grad_before_b, w_fc1)
        grad_norm_two = lax.psum(norm_two_part.astype(jnp.bfloat16), "tensor").astype(jnp.float32)
        delta_gain_two = jnp.sum(grad_norm_two * scaled_two, axis=0)
        delta_shift_two = jnp.sum(grad_norm_two, axis=0)
        grad_resid = grad_out + norm_back(
            grad_norm_two, scaled_two, inverse_two, gain_two.astype(jnp.float32)
        )
        delta_proj_bias = jnp.sum(grad_resid, axis=0)
        grad_resid_b = grad_resid.astype(jnp.bfloat16)
        delta_proj_weight = inner_rows(context, grad_resid_b)
        grad_context = outer_cols(grad_resid_b, w_proj).astype(jnp.bfloat16)
        grad_context = grad_context.reshape(slots, seq_len, heads_here, HD)
        again = (
            jnp.einsum("gqhe,gkhe->ghqk", query, keys_all, preferred_element_type=jnp.float32)
            * scale
        )
        weights_again = jnp.exp(again - log_total[..., None])
        probs_again = weights_again.astype(jnp.bfloat16)
        grad_probs = jnp.einsum(
            "gqhe,gkhe->ghqk", grad_context, values_all, preferred_element_type=jnp.float32
        )
        row_dot = jnp.sum(weights_again * grad_probs, axis=-1, keepdims=True)
        grad_scores = (weights_again * (grad_probs - row_dot) * scale).astype(jnp.bfloat16)
        grad_query = jnp.einsum(
            "ghqk,gkhe->gqhe", grad_scores, keys_all, preferred_element_type=jnp.float32
        )
        grad_keys = jnp.einsum(
            "ghqk,gqhe->gkhe", grad_scores, query, preferred_element_type=jnp.float32
        )
        grad_values = jnp.einsum(
            "ghqk,gqhe->gkhe", probs_again, grad_context, preferred_element_type=jnp.float32
        )
        grad_mixed = jnp.stack(
            [
                grad_query.reshape(row_count, group_cols),
                grad_keys.reshape(row_count, group_cols),
                grad_values.reshape(row_count, group_cols),
            ],
            axis=1,
        )
        delta_qkv_bias = jnp.stack(
            [jnp.sum(grad_mixed[:, 0], axis=0), jnp.sum(grad_mixed[:, 2], axis=0)]
        )
        grad_mixed_b = grad_mixed.astype(jnp.bfloat16).reshape(row_count, 3 * group_cols)
        delta_qkv_weight = inner_rows(normed_one, grad_mixed_b).reshape(width, 3, group_cols)
        norm_one_part = outer_cols(grad_mixed_b, w_qkv.reshape(width, 3 * group_cols))
        grad_norm_one = lax.psum(norm_one_part.astype(jnp.bfloat16), "tensor").astype(jnp.float32)
        delta_gain_one = jnp.sum(grad_norm_one * scaled_one, axis=0)
        delta_shift_one = jnp.sum(grad_norm_one, axis=0)
        grad_input = grad_resid + norm_back(
            grad_norm_one, scaled_one, inverse_one, gain_one.astype(jnp.float32)
        )
        in_grads.append(grad_input.reshape(slots, seq_len, width))
        terms = (
            delta_gain_one,
            delta_shift_one,
            delta_qkv_weight,
            delta_qkv_bias,
            delta_proj_weight,
            delta_proj_bias,
            delta_gain_two,
            delta_shift_two,
            delta_fc1_weight,
            delta_fc1_bias,
            delta_fc2_weight,
            delta_fc2_bias,
        )
        if totals is None:
            totals = terms
        else:
            totals = tuple(jax.tree.map(lambda total, term: total + term, totals, terms))
    owned = (
        lax.psum_scatter(totals[0], "dp", scatter_dimension=0, tiled=True),
        lax.psum_scatter(totals[1], "dp", scatter_dimension=0, tiled=True),
        lax.psum_scatter(totals[2], "dp", scatter_dimension=0, tiled=True),
        lax.psum_scatter(totals[3], "dp", scatter_dimension=1, tiled=True),
        lax.psum_scatter(totals[4], "dp", scatter_dimension=1, tiled=True),
        lax.psum_scatter(totals[5], "dp", scatter_dimension=0, tiled=True),
        lax.psum_scatter(totals[6], "dp", scatter_dimension=0, tiled=True),
        lax.psum_scatter(totals[7], "dp", scatter_dimension=0, tiled=True),
        lax.psum_scatter(totals[8], "dp", scatter_dimension=0, tiled=True),
        lax.psum_scatter(totals[9], "dp", scatter_dimension=0, tiled=True),
        lax.psum_scatter(totals[10], "dp", scatter_dimension=1, tiled=True),
        lax.psum_scatter(totals[11], "dp", scatter_dimension=0, tiled=True),
    )
    activations = jnp.stack(outputs)
    input_grad = jnp.stack(in_grads)
    return (
        activations,
        input_grad,
        owned[0],
        owned[1],
        owned[2],
        owned[3],
        owned[4],
        owned[5],
        owned[6],
        owned[7],
        owned[8],
        owned[9],
        owned[10],
        owned[11],
    )


def solution(mesh):
    in_specs = (
        P(None, "dp", None, None),
        P(None, "dp"),
        P("dp"),
        P("dp"),
        P("dp", None, "tensor"),
        P(None, ("tensor", "dp")),
        P("tensor", "dp"),
        P("dp"),
        P("dp"),
        P("dp"),
        P("dp", "tensor"),
        P(("tensor", "dp")),
        P("tensor", "dp"),
        P("dp"),
        P(None, "dp", None, None),
    )
    out_specs = (
        P(None, "dp", None, None),
        P(None, "dp", None, None),
        P("dp"),
        P("dp"),
        P("dp", None, "tensor"),
        P(None, ("tensor", "dp")),
        P("tensor", "dp"),
        P("dp"),
        P("dp"),
        P("dp"),
        P("dp", "tensor"),
        P(("tensor", "dp")),
        P("tensor", "dp"),
        P("dp"),
    )
    return jax.shard_map(
        per_device, mesh=mesh, in_specs=in_specs, out_specs=out_specs, check_vma=False
    )
```

profile of v0, /device:TPU:0, one launch (start us, length us, event | category | flops | bytes accessed | tf_op | source)
XLA Modules:
  0.0 1305.1 jit_solution(14810016866845030985)
XLA Ops:
  16.5 79.1 %all-reduce.16 = (bf16[768]{0:T(1024)(128)(2,1)S(1)}, bf16[768]{0:T(1024)(128)(2,1)S(1)}, bf16[768]{0:T(1024)(128)(2,1)S(1)}, bf16[1536]{0:T(1024)(128)(2,1)S(1)...) all-reduce(bf16[768]{0:T(1024)(128)(2,1)S(1)} %dynamic-update-slice, ...), channel_id=1, replica_groups=mesh['dp'=16,'tensor'=2] {'dp'}, use_global_device_ids=true, to_apply=%add.1 | all-reduce | flops 6144 | bytes 24576
  95.6 14.5 %convert_reduce_fusion.8 = (f32[6,197]{1,0:T(8,128)S(1)}, f32[6,197]{1,0:T(8,128)S(1)}) fusion(bf16[2,6,197,768]{3,0,2,1:T(2,128)(2,1)} %param.15), kind=kLoop, calls=%fused_computation.138 | loop fusion | flops 3628740 | bytes 3640560 | tf_op jit(solution)/shard_map/reduce_sum | solution.py:13
  110.2 42.6 %multiply_reduce_fusion.7 = (f32[6,197]{1,0:T(8,128)S(1)}, f32[6,197]{1,0:T(8,128)S(1)}, f32[6,197,768]{2,1,0:T(8,128)}, f32[6,197,768]{2,1,0:T(8,128)}) fusion(f32[6,197]{1,0:T(8,128)S(1)} %get-tuple-element.145, bf16[2,6,197,768]{3,0,2,1:T(2,128)(2,1)S(1)} %copy-done, f32[6,197]{1,0:T(8,128)S(1)} %get-tuple-element.144), kind=kLoop, calls=%fused_computation.143 | loop fusion | flops 7259844 | bytes 10912224 | tf_op jit(solution)/shard_map/reduce_sum | solution.py:15
  152.8 31.7 %convert_reduce_fusion.11 = (bf16[6,197,768]{2,1,0:T(8,128)(2,1)}, bf16[6,197,768]{2,1,0:T(8,128)(2,1)S(1)}) fusion(f32[768]{0:T(1024)S(1)} %convert_element_type.254, f32[768]{0:T(1024)S(1)} %convert_element_type.253, f32[6,197]{1,0:T(8,128)S(1)} %add_rsqrt_fusion.3, f32[6,197]{1,0:T(8,128)S(1)} %get-tuple-element.145, bf16[2,6,197,768]{3,0,2,1:T(2,128)(2,1)} %param.15, ...), kind=kLoop, calls=%fused_computation.142 | loop fusion | flops 10893312 | bytes 7287264 | tf_op jit(solution)/shard_map/convert_element_type | solution.py:107
  187.8 35.5 %all-gather = bf16[16,24,2]{1,2,0:T(2,128)(2,1)S(1)} all-gather(bf16[1,24,2]{1,2,0:T(2,128)(2,1)S(1)} %bitcast.124), channel_id=1, replica_groups=mesh['dp'=16,'tensor'=2] {'dp'}, dimensions={0}, use_global_device_ids=true | all-gather | bytes 1632 | tf_op jit(solution)/shard_map/all_gather | solution.py:73
  225.3 41.4 %all_gather.28 = bf16[384,768]{0,1:T(8,128)(2,1)S(1)} all-gather(bf16[384,48]{0,1:T(8,128)(2,1)S(1)} %copy-done.64), channel_id=1, replica_groups=mesh['dp'=16,'tensor'=2] {'dp'}, dimensions={1}, use_global_device_ids=true | all-gather | bytes 626688 | tf_op jit(solution)/shard_map/all_gather | solution.py:74
  362.7 39.9 %fusion.82 = (f32[768]{0:T(1024)}, f32[768]{0:T(1024)}, f32[6,197,768]{2,1,0:T(8,128)}, f32[6,197,768]{2,1,0:T(8,128)}) fusion(bf16[2,6,197,768]{3,0,2,1:T(2,128)(2,1)} %param.29, f32[6]{0:T(128)S(1)} %get-tuple-element.146, f32[6]{0:T(128)S(1)} %get-tuple-element.147), kind=kLoop, calls=%fused_computation.130 | loop fusion | flops 5445120 | bytes 10899504 | tf_op jit(solution)/shard_map/reduce_sum | solution.py:152
  420.4 15.8 %all-gather.7.cloned.1.call-done = bf16[768,1536]{1,0:T(8,128)(2,1)} async-done(((bf16[48,1536]{1,0:T(8,128)(2,1)}), bf16[768,1536]{1,0:T(8,128)(2,1)}) %all-gather.7.cloned.1.call-update) | async-done | bytes 2359312 | tf_op jit(solution)/shard_map/all_gather | solution.py:78
  436.2 22.7 %multiply_convert_fusion.3 = (bf16[1182,1536]{1,0:T(8,128)(2,1)}, f32[1182,1536]{1,0:T(8,128)}, f32[1182,1536]{1,0:T(8,128)}) fusion(f32[1536]{0:T(1024)S(1)} %convert_element_type.268, bf16[768,1536]{1,0:T(8,128)(2,1)} %all-gather.7.cloned.1.call-done, f32[1182,768]{1,0:T(8,128)} %copy-done.7, f32[768]{0:T(1024)S(1)} %convert_element_type.266, ...), kind=kOutput, calls=%fused_computation.34 | convolution fusion | flops 2913053184 | bytes 24167664 | tf_op jit(solution)/shard_map/dot_general | solution.py:133
  459.0 20.8 %multiply_convert_fusion.2 = (bf16[1182,1536]{1,0:T(8,128)(2,1)}, f32[1182,1536]{1,0:T(8,128)}, f32[1182,1536]{1,0:T(8,128)}) fusion(f32[1536]{0:T(1024)S(1)} %convert_element_type.268, bf16[768,1536]{1,0:T(8,128)(2,1)S(1)} %copy-done.84, f32[1182,768]{1,0:T(8,128)S(1)} %copy-done.4, f32[1182]{0:T(1024)S(1)} %add_rsqrt_fusion, ...), kind=kOutput, calls=%fused_computation.21 | convolution fusion | flops 2913053184 | bytes 24167664 | tf_op jit(solution)/shard_map/dot_general | solution.py:133
  479.8 19.7 %all-gather.9.cloned.1.call-done = bf16[1536,768]{0,1:T(8,128)(2,1)} async-done(((bf16[1536,48]{0,1:T(8,128)(2,1)}), bf16[1536,768]{0,1:T(8,128)(2,1)}) %all-gather.9.cloned.1.call-update) | async-done | bytes 2359312 | tf_op jit(solution)/shard_map/all_gather | solution.py:80
  499.5 11.4 fusion.163
  542.7 12.2 all-reduce.26.cloned.1.call-done
  583.7 15.1 %fusion.160 = (f32[6,64]{1,0:T(8,128)}, bf16[6,197,6,64]{1,3,2,0:T(8,128)(2,1)}) fusion(bf16[6,197,6,64]{1,3,2,0:T(8,128)(2,1)} %copy.126, f32[6,6,197,197]{2,3,1,0:T(8,128)} %fusion.166, f32[6,6,197,197]{2,3,1,0:T(8,128)} %copy-done.2, f32[6,6,197]{2,1,0:T(8,128)S(1)} %copy-done.43), kind=kOutput, calls=%fused_computation.238 | convolution fusion | flops 192320672 | bytes 13022448 | tf_op jit(solution)/shard_map/ghqk,gkhe->gqhe/dot_general | solution.py:182
  598.8 12.6 fusion.103
  629.2 14.7 %fusion.156 = (f32[6,64]{1,0:T(8,128)}, bf16[6,197,6,64]{1,3,2,0:T(8,128)(2,1)}) fusion(bf16[6,197,6,64]{1,3,2,0:T(8,128)(2,1)S(1)} %copy-done.25, f32[6,6,197,197]{2,3,1,0:T(8,128)} %fusion.165, f32[6,6,197,197]{2,3,1,0:T(8,128)} %copy-done.1, f32[6,6,197]{2,1,0:T(8,128)} %copy-done.40), kind=kOutput, calls=%fused_computation.236 | convolution fusion | flops 192320672 | bytes 13022448 | tf_op jit(solution)/shard_map/ghqk,gkhe->gqhe/dot_general | solution.py:182
  643.9 12.7 fusion.109
  763.4 77.5 %all-reduce.15 = (f32[768]{0:T(1024)S(1)}, f32[768]{0:T(1024)S(1)}, f32[2,384]{1,0:T(2,128)S(1)}, f32[768]{0:T(1024)S(1)}, f32[768]{0:T(1024)S(1)}, /*index=5*/f...) all-reduce(f32[768]{0:T(1024)S(1)} %add.270, ...), channel_id=2, replica_groups=mesh['dp'=16,'tensor'=2] {'dp'}, use_global_device_ids=true, to_apply=%region_32.0.clone | all-reduce | flops 6912 | bytes 55296
  865.0 11.7 copy.166
  882.5 11.1 stack_reshape.40
  897.4 12.6 pad_maximum_fusion.1
  910.0 105.7 %reduce-scatter.10.cloned.1.call-done = f32[48,1536]{1,0:T(8,128)} async-done(((f32[768,1536]{1,0:T(8,128)}), f32[48,1536]{1,0:T(8,128)}) %reduce-scatter.10.cloned.1.call-update) | async-done | bytes 294928 | tf_op jit(solution)/shard_map/reduce_scatter | solution.py:239
  1015.8 143.2 %reduce-scatter.12.cloned.1.call-done = f32[1536,48]{0,1:T(8,128)} async-done(((f32[1536,768]{0,1:T(8,128)}), f32[1536,48]{0,1:T(8,128)}) %reduce-scatter.12.cloned.1.call-update) | async-done | bytes 294928 | tf_op jit(solution)/shard_map/reduce_scatter | solution.py:241
  1159.0 139.1 %reduce-scatter.6.cloned.1.call-done = f32[48,3,384]{2,0,1:T(8,128)} async-done(((f32[768,3,384]{2,0,1:T(8,128)}), f32[48,3,384]{2,0,1:T(8,128)}) %reduce-scatter.6.cloned.1.call-update) | async-done | bytes 221200 | tf_op jit(solution)/shard_map/reduce_scatter | solution.py:233
  (370 shorter events, 342.5 us)
Async XLA Ops:
  7.2 259.6 %all-gather.5.cloned.1.call-start = ((), (), s32[]{:S(2)}) async-start(), calls=%async_computation.4 | async-start | bytes 1880064 | tf_op jit(solution)/shard_map/all_gather | solution.py:72
  7.9 404.2 %all-reduce.28.cloned.1.call-start = ((), (), s32[]{:S(2)}) async-start(), calls=%async_computation.13 | async-start | bytes 7274496 | tf_op jit(solution)/shard_map/psum | solution.py:127
  95.6 57.2 %copy-start.48 = (f32[768]{0:T(1024)}, f32[768]{0:T(1024)S(1)}, u32[]{:S(2)}) copy-start(f32[768]{0:T(1024)S(1)} %convert_element_type.253) | copy-start | bytes 9220
  110.1 42.6 %copy-start.44 = (f32[6,197]{1,0:T(8,128)}, f32[6,197]{1,0:T(8,128)S(1)}, u32[]{:S(2)}) copy-start(f32[6,197]{1,0:T(8,128)S(1)} %get-tuple-element.144) | copy-start | bytes 14188
  110.1 42.6 %copy-start.46 = (f32[6,197]{1,0:T(8,128)}, f32[6,197]{1,0:T(8,128)S(1)}, u32[]{:S(2)}) copy-start(f32[6,197]{1,0:T(8,128)S(1)} %get-tuple-element.145) | copy-start | bytes 14188
  152.7 31.8 %copy-start.58 = (f32[6,197]{1,0:T(8,128)}, f32[6,197]{1,0:T(8,128)S(1)}, u32[]{:S(2)}) copy-start(f32[6,197]{1,0:T(8,128)S(1)} %add_rsqrt_fusion.1) | copy-start | bytes 14188
  152.8 31.7 %copy-start.60 = (f32[6,197]{1,0:T(8,128)}, f32[6,197]{1,0:T(8,128)S(1)}, u32[]{:S(2)}) copy-start(f32[6,197]{1,0:T(8,128)S(1)} %add_rsqrt_fusion.3) | copy-start | bytes 14188
  184.5 40.8 %copy-start.64 = (bf16[384,48]{0,1:T(8,128)(2,1)S(1)}, bf16[384,48]{0,1:T(8,128)(2,1)}, u32[]{:S(2)}) copy-start(bf16[384,48]{0,1:T(8,128)(2,1)} %param.21) | copy-start | bytes 110596
  225.2 45.7 %copy-start.32 = (bf16[1182,768,1]{1,0,2:T(8,128)(2,1)S(1)}, bf16[1182,768,1]{1,0,2:T(8,128)(2,1)}, u32[]{:S(2)}) copy-start(bf16[1182,768,1]{1,0,2:T(8,128)(2,1)} %reshape.430) | copy-start | bytes 5446660
  266.7 80.5 %copy-start.22 = (bf16[384,768]{0,1:T(8,128)(2,1)}, bf16[384,768]{0,1:T(8,128)(2,1)S(1)}, u32[]{:S(2)}) copy-start(bf16[384,768]{0,1:T(8,128)(2,1)S(1)} %all_gather.28) | copy-start | bytes 1769476
  349.7 86.6 %all-gather.7.cloned.1.call-start = ((), (), s32[]{:S(2)}) async-start(), calls=%async_computation.5 | async-start | bytes 2506752 | tf_op jit(solution)/shard_map/all_gather | solution.py:78
  350.4 149.1 %all-gather.9.cloned.1.call-start = ((), (), s32[]{:S(2)}) async-start(), calls=%async_computation.6 | async-start | bytes 2506752 | tf_op jit(solution)/shard_map/all_gather | solution.py:80
  351.0 203.9 %all-reduce.26.cloned.1.call-start = ((), (), s32[]{:S(2)}) async-start(), calls=%async_computation.12 | async-start | bytes 7274496 | tf_op jit(solution)/shard_map/psum | solution.py:160
  360.8 207.5 %copy-start.62 = (f32[768]{0:T(1024)}, f32[768]{0:T(1024)S(1)}, u32[]{:S(2)}) copy-start(f32[768]{0:T(1024)S(1)} %convert_element_type.265) | copy-start | bytes 9220
  360.8 98.2 %copy-start.76 = (f32[768]{0:T(1024)}, f32[768]{0:T(1024)S(1)}, u32[]{:S(2)}) copy-start(f32[768]{0:T(1024)S(1)} %convert_element_type.266) | copy-start | bytes 9220
  407.1 152.8 %copy-start.50 = (f32[1182]{0:T(1024)}, f32[1182]{0:T(1024)S(1)}, u32[]{:S(2)}) copy-start(f32[1182]{0:T(1024)S(1)} %broadcast_in_dim.9) | copy-start | bytes 14188
  418.0 141.9 %copy-start.54 = (f32[1182]{0:T(1024)}, f32[1182]{0:T(1024)S(1)}, u32[]{:S(2)}) copy-start(f32[1182]{0:T(1024)S(1)} %add_rsqrt_fusion.2) | copy-start | bytes 14188
  420.4 147.8 %copy-start.56 = (f32[1182]{0:T(1024)}, f32[1182]{0:T(1024)S(1)}, u32[]{:S(2)}) copy-start(f32[1182]{0:T(1024)S(1)} %add_rsqrt_fusion) | copy-start | bytes 14188
  532.0 219.4 %all-reduce.24.cloned.1.call-start = ((), (), s32[]{:S(2)}) async-start(), calls=%async_computation.11 | async-start | bytes 14548992 | tf_op jit(solution)/shard_map/psum | solution.py:138
  704.9 205.1 %reduce-scatter.8.cloned.1.call-start = ((), (), s32[]{:S(2)}) async-start(), calls=%async_computation.8 | async-start | bytes 1253376 | tf_op jit(solution)/shard_map/reduce_scatter | solution.py:235
  711.9 303.9 %reduce-scatter.10.cloned.1.call-start = ((), (), s32[]{:S(2)}) async-start(), calls=%async_computation.9 | async-start | bytes 5013504 | tf_op jit(solution)/shard_map/reduce_scatter | solution.py:239
  725.2 433.8 %reduce-scatter.12.cloned.1.call-start = ((), (), s32[]{:S(2)}) async-start(), calls=%async_computation.10 | async-start | bytes 5013504 | tf_op jit(solution)/shard_map/reduce_scatter | solution.py:241
  738.1 560.0 %reduce-scatter.6.cloned.1.call-start = ((), (), s32[]{:S(2)}) async-start(), calls=%async_computation.7 | async-start | bytes 3760128 | tf_op jit(solution)/shard_map/reduce_scatter | solution.py:233
  755.9 88.6 %copy-start.21 = (bf16[1182,768]{1,0:T(8,128)(2,1)S(1)}, bf16[1182,768]{1,0:T(8,128)(2,1)}, u32[]{:S(2)}) copy-start(bf16[1182,768]{1,0:T(8,128)(2,1)} %get-tuple-element.87) | copy-start | bytes 5446660
  (78 other events, 424.7 us)
Sparse Core Ops, SparseCore 0:
  10.7 62.0 all-gather.4
  349.8 20.1 all-reduce.27
  372.8 63.3 all-gather.6
  438.9 60.5 all-gather.8
  532.2 22.6 all-reduce.25
  705.0 35.4 all-reduce.23
  745.8 126.1 reduce-scatter.7
  877.8 137.8 reduce-scatter.9
  1021.5 137.4 reduce-scatter.11
  1164.5 133.5 reduce-scatter.5
where the time goes:
time: 1320 us; the launch traced here: 1310 us
  waiting for transfers between devices  438 us (33%)
  matrix products  242 us (18%)
  blocking collectives  234 us (18%)
  other arithmetic  197 us (15%)
  local copies, waits for them, and re-layouts  175 us (13%)
  between operations  19 us (1%)
    unnamed x2, blocking collectives  157 us
    reduce_scatter x1, waiting for transfers between devices, per_device(): lax.psum_scatter(totals[10], 'dp', scatter_dimension=1, tiled=True)  143 us
    reduce_scatter x1, waiting for transfers between devices, per_device(): lax.psum_scatter(totals[2], 'dp', scatter_dimension=0, tiled=True)  139 us
    reduce_scatter x1, waiting for transfers between devices, per_device(): lax.psum_scatter(totals[8], 'dp', scatter_dimension=0, tiled=True)  106 us
    reduce_sum x3, other arithmetic, layer_norm(): variance = jnp.mean(offset * offset, axis=-1, keepdims=True)  43.7 us
    dot_general x2, matrix products, per_device(): jnp.dot(normed_two, w_fc1, preferred_element_type=jnp.float32)  43.5 us
    all_gather x1, blocking collectives, per_device(): lax.all_gather(proj_weight, 'dp', axis=1, tiled=True)  41.4 us
    dot_general x8, matrix products, inner_rows(): lax.dot_general(operand, factor, (((0,), (0,)), ((), ())), preferred_elem...  40.7 us
  transfers between devices with their start and end apart: 10, of which 6 were waited for; matrix products, arithmetic and copies ran while one was open for 26% of the time, Pallas kernels for 0%

commit v1 on v0

v1 whole, which is shorter than its diff:
```python
import functools
import math

import jax
import jax.numpy as jnp
from jax import lax
from jax.experimental import pallas as pl
from jax.experimental.pallas import tpu as pltpu
from jax.sharding import PartitionSpec as P

HD = 64
EPS = 1e-06
BF = jnp.bfloat16
F32 = jnp.float32
ROW_TILE = 16
LANES = 128
BATCH = 2
CHUNKS = 3
VMEM_LIMIT = 60 * 1024 * 1024

ERFC = (
    0.16918800397535036,
    0.17071524523359413,
    0.14833905737234418,
    0.21492644132531408,
    -0.09465150833103098,
    0.5477210173469333,
    -0.5122788444212757,
    0.4855635302821805,
    -0.1295229623684681,
)
ERFC_HALF = tuple(0.5 * c for c in ERFC)
T_SCALE = 0.3 / math.sqrt(2.0)
PHI_SCALE = 1.0 / math.sqrt(2.0 * math.pi)


def gelu_pair(v):
    t = 1.0 / (1.0 + T_SCALE * jnp.abs(v))
    acc = jnp.full_like(v, ERFC_HALF[-1])
    for c in ERFC_HALF[-2::-1]:
        acc = acc * t + c
    e = jnp.exp(-0.5 * v * v)
    tail = acc * t * e
    cdf = jnp.where(v >= 0, 1.0 - tail, tail)
    return v * cdf, cdf + v * (PHI_SCALE * e)


def nt(a, b):
    return lax.dot_general(a, b, (((1,), (1,)), ((), ())), preferred_element_type=F32)


def tn(a, b):
    return lax.dot_general(a, b, (((0,), (0,)), ((), ())), preferred_element_type=F32)


def nn(a, b):
    return jnp.dot(a, b, preferred_element_type=F32)


def norm_stats(x):
    center = jnp.mean(x, axis=-1, keepdims=True)
    offset = x - center
    inverse = lax.rsqrt(jnp.mean(offset * offset, axis=-1, keepdims=True) + EPS)
    return offset * inverse, inverse


def norm_back(g, scaled, inverse, gain):
    u = g * gain
    first = jnp.mean(u, axis=-1, keepdims=True)
    second = jnp.mean(u * scaled, axis=-1, keepdims=True)
    return inverse * (u - first - scaled * second)


def fold8(x):
    return jnp.sum(x.reshape(x.shape[0] // 8, 8, x.shape[1]), axis=0)


def add_to(ref, value):
    @pl.when(pl.program_id(0) == 0)
    def _():
        ref[...] = value

    @pl.when(pl.program_id(0) > 0)
    def _():
        ref[...] += value


def load_weights(table, sources, w, sem):
    copies = []
    k = 0
    cols = w.shape[1] // len(sources)
    for h, arrays in enumerate(sources):
        for src in arrays:
            blocks, rows, _ = src.shape
            for s in range(blocks):
                row = pl.multiple_of(table[k] * rows, ROW_TILE)
                copies.append(
                    pltpu.make_async_copy(
                        src.at[s], w.at[pl.ds(row, rows), pl.ds(h * cols, cols)], sem.at[k]
                    )
                )
                k += 1
    return copies


def split_sources(refs, per_half):
    return refs[:per_half], refs[per_half : 2 * per_half]


def attn_fwd_kernel(seq, per_half, table, x_ref, vec_ref, *refs):
    sources = split_sources(refs, per_half)
    normed_ref, qkv_ref, lse_ref, ctx_ref, w, sem = refs[2 * per_half :]
    copies = load_weights(table, sources, w, sem)
    first = pl.program_id(0) == 0

    @pl.when(first)
    def _():
        for c in copies:
            c.start()

    width = x_ref.shape[1]
    cols = qkv_ref.shape[2]
    group = cols // 3
    scaled, _ = norm_stats(x_ref[...].astype(F32))
    normed = (scaled * vec_ref[0:1, :width] + vec_ref[1:2, :width]).astype(BF)
    normed_ref[...] = normed

    @pl.when(first)
    def _():
        for c in copies:
            c.wait()

    for h in range(2):
        part = nn(normed, w[:, h * cols : (h + 1) * cols]) + vec_ref[7:8, h * cols : (h + 1) * cols]
        qkv_ref[h] = part.astype(BF)

    tall = x_ref.shape[0] // BATCH
    lane = lax.broadcasted_iota(jnp.int32, (tall, LANES), 1)
    low = lane < HD
    keep = lax.broadcasted_iota(jnp.int32, (tall, tall), 1) < seq

    def one(step, carry):
        image, h = step // 2, step % 2
        rows = pl.ds(pl.multiple_of(image * tall, ROW_TILE), tall)
        logs = jnp.zeros((tall, LANES), F32)
        for pair in range(group // LANES):
            at = pair * LANES
            q = qkv_ref[h, rows, at : at + LANES] * 0.125
            k = qkv_ref[h, rows, group + at : group + at + LANES]
            v = qkv_ref[h, rows, 2 * group + at : 2 * group + at + LANES]
            outs = []
            for e in range(2):
                mine = low if e == 0 else ~low
                s = nt(jnp.where(mine, q, jnp.zeros_like(q)), k)
                s = jnp.where(keep, s, -1e30)
                top = jnp.max(s, axis=-1, keepdims=True)
                p = jnp.exp(s - top)
                total = jnp.sum(p, axis=-1, keepdims=True)
                logs = jnp.where(lane == 2 * pair + e, top + jnp.log(total), logs)
                probs = (p * (1.0 / total)).astype(BF)
                outs.append(nn(probs, v))
            ctx_ref[h, rows, at : at + LANES] = jnp.where(low, outs[0], outs[1]).astype(BF)
        lse_ref[h, rows, :] = logs
        return carry

    lax.fori_loop(0, 2 * BATCH, one, 0)


def mlp_fwd_kernel(per_half, table, live, ctx_ref, x_ref, vec_ref, *refs):
    sources = split_sources(refs, per_half)
    resid_ref, normed_ref, hidden_ref, slope_ref, act_ref, w, sem, acc = refs[2 * per_half :]
    copies = load_weights(table, sources, w, sem)
    step = pl.program_id(0)

    @pl.when(step == 0)
    def _():
        for c in copies:
            c.start()
        for c in copies:
            c.wait()

    rows, width = x_ref.shape
    cols = w.shape[1] // 2
    group, ff = ctx_ref.shape[2], hidden_ref.shape[2]
    attn = nt(ctx_ref[0], w[:, :group]) + nt(ctx_ref[1], w[:, cols : cols + group])
    resid = x_ref[...].astype(F32) + attn + vec_ref[2:3, :width]
    resid_ref[...] = resid
    scaled, _ = norm_stats(resid)
    normed_ref[...] = (scaled * vec_ref[3:4, :width] + vec_ref[4:5, :width]).astype(BF)
    chunk = ff // CHUNKS

    def one(step, carry):
        h, c = step // CHUNKS, step % CHUNKS
        at = pl.multiple_of(h * cols + group + c * chunk, LANES)
        here = pl.ds(pl.multiple_of(c * chunk, LANES), chunk)
        bias = vec_ref[6:7, pl.ds(pl.multiple_of(step * chunk, LANES), chunk)]
        value, slope = gelu_pair(nn(normed_ref[...], w[:, pl.ds(at, chunk)]) + bias)
        hidden = value.astype(BF)
        hidden_ref[h, :, here] = hidden
        slope_ref[h, :, here] = slope.astype(BF)
        acc[...] += nt(hidden, w[:, pl.ds(pl.multiple_of(at + ff, LANES), chunk)])
        return carry

    acc[...] = resid
    lax.fori_loop(0, 2 * CHUNKS, one, 0)
    image = lax.broadcasted_iota(jnp.int32, (rows, 1), 0) // (rows // BATCH)
    alive = jnp.zeros((rows, 1), F32)
    for i in range(BATCH):
        alive = jnp.where(image == i, live[step * BATCH + i].astype(F32), alive)
    act_ref[...] = ((acc[...] + vec_ref[5:6, :width]) * alive).astype(BF)


def mlp_bwd_kernel(per_half, table, go_ref, slope_ref, resid_ref, vec_ref, *refs):
    sources = split_sources(refs, per_half)
    gpre_ref, gr_ref, grb_ref, gctx_ref, small_ref, fc1b_ref, w, sem = refs[2 * per_half :]
    copies = load_weights(table, sources, w, sem)
    step = pl.program_id(0)

    @pl.when(step == 0)
    def _():
        fc1b_ref[...] = jnp.zeros_like(fc1b_ref)
        for c in copies:
            c.start()
        for c in copies:
            c.wait()

    rows, width = go_ref.shape
    cols = w.shape[1] // 2
    group, ff = gctx_ref.shape[2], gpre_ref.shape[2]
    chunk = ff // 3

    def one(h, acc):
        for c in range(3):
            at = pl.multiple_of(h * cols + group + c * chunk, LANES)
            gh = nn(go_ref[...], w[:, pl.ds(pl.multiple_of(at + ff, LANES), chunk)])
            gpre = gh * slope_ref[h, :, c * chunk : (c + 1) * chunk].astype(F32)
            where = pl.ds(pl.multiple_of(h * ff + c * chunk, LANES), chunk)
            fc1b_ref[:, where] += fold8(gpre)
            gpre = gpre.astype(BF)
            gpre_ref[h, :, c * chunk : (c + 1) * chunk] = gpre
            acc = acc + nt(gpre, w[:, pl.ds(at, chunk)])
        return acc

    gn = lax.fori_loop(0, 2, one, jnp.zeros((rows, width), F32))
    scaled, inverse = norm_stats(resid_ref[...])
    go = go_ref[...].astype(F32)
    gr = go + norm_back(gn, scaled, inverse, vec_ref[3:4, :width])
    gr_ref[...] = gr
    grb = gr.astype(BF)
    grb_ref[...] = grb
    for h in range(2):
        gctx_ref[h] = nn(grb, w[:, h * cols : h * cols + group]).astype(BF)
    add_to(
        small_ref,
        jnp.concatenate([fold8(gn * scaled), fold8(gn), fold8(gr), fold8(go)], axis=0),
    )


def attn_bwd_kernel(seq, per_half, table, qkv_ref, lse_ref, gctx_ref, x_ref, gr_ref, vec_ref, *refs):
    sources = split_sources(refs, per_half)
    gqkv_ref, gin_ref, small_ref, bias_ref, w, sem = refs[2 * per_half :]
    copies = load_weights(table, sources, w, sem)
    first = pl.program_id(0) == 0

    @pl.when(first)
    def _():
        bias_ref[...] = jnp.zeros_like(bias_ref)
        for c in copies:
            c.start()

    rows, width = x_ref.shape
    cols = qkv_ref.shape[2]
    group = cols // 3
    tall = rows // BATCH
    lane = lax.broadcasted_iota(jnp.int32, (tall, LANES), 1)
    low = lane < HD
    keep = lax.broadcasted_iota(jnp.int32, (tall, tall), 1) < seq

    pairs = group // LANES

    def one(step, carry):
        image, h, pair = step // (2 * pairs), step // pairs % 2, step % pairs
        at_rows = pl.ds(pl.multiple_of(image * tall, ROW_TILE), tall)
        at = pair * LANES
        cols_of = [pl.ds(pl.multiple_of(part * group + at, LANES), LANES) for part in range(3)]
        logs = lse_ref[h, at_rows, :]
        q = qkv_ref[h, at_rows, cols_of[0]] * 0.125
        k = qkv_ref[h, at_rows, cols_of[1]]
        v = qkv_ref[h, at_rows, cols_of[2]]
        g = gctx_ref[h, at_rows, cols_of[0]]
        got = []
        for e in range(2):
            mine = low if e == 0 else ~low
            s = nt(jnp.where(mine, q, jnp.zeros_like(q)), k)
            lse = jnp.sum(jnp.where(lane == 2 * pair + e, logs, 0.0), axis=-1, keepdims=True)
            weights = jnp.exp(jnp.where(keep, s - lse, -1e30))
            gp = nt(jnp.where(mine, g, jnp.zeros_like(g)), v)
            wg = weights * gp
            dot = jnp.sum(wg, axis=-1, keepdims=True)
            gs = (wg - weights * dot).astype(BF)
            got.append((nn(gs, k), tn(gs, q), tn(weights.astype(BF), g)))
        gq, gk, gv = (jnp.where(low, a, b) for a, b in zip(*got))
        gq = gq * 0.125
        for to, value in zip(cols_of, (gq, gk, gv)):
            gqkv_ref[h, at_rows, to] = value.astype(BF)
        bias_ref[h, 0:8, cols_of[0]] += fold8(gq)
        bias_ref[h, 8:16, cols_of[0]] += fold8(gv)
        return carry

    lax.fori_loop(0, 2 * BATCH * pairs, one, 0)

    @pl.when(first)
    def _():
        for c in copies:
            c.wait()

    gn = nt(gqkv_ref[0], w[:, :cols]) + nt(gqkv_ref[1], w[:, cols:])
    scaled, inverse = norm_stats(x_ref[...].astype(F32))
    gin = gr_ref[...] + norm_back(gn, scaled, inverse, vec_ref[0:1, :width])
    gin_ref[...] = gin.astype(BF)
    add_to(small_ref, jnp.concatenate([fold8(gn * scaled), fold8(gn)], axis=0))


SMEM_SPEC = pl.BlockSpec(memory_space=pltpu.SMEM)
ANY_SPEC = pl.BlockSpec(memory_space=pl.ANY)


def row_spec(step_rows, shape):
    if len(shape) == 2:
        return pl.BlockSpec((step_rows, shape[1]), lambda i: (i, 0))
    return pl.BlockSpec((shape[0], step_rows, shape[2]), lambda i: (0, i, 0))


def whole_spec(shape):
    return pl.BlockSpec(shape, lambda i: (0,) * len(shape))


def run(kernel, name, steps, step_rows, scalars, rows_in, whole_in, sources, rows_out, whole_out, w_cols, flops, extra=()):
    flat = [a for half in sources for a in half]
    n_copies = sum(a.shape[0] for a in flat)
    width = sum(a.shape[0] * a.shape[1] for a in sources[0])
    out_shape = [jax.ShapeDtypeStruct(s, d) for s, d in rows_out + whole_out]
    moved = sum(a.size * a.dtype.itemsize for a in rows_in + flat)
    moved += sum(math.prod(s) * jnp.dtype(d).itemsize for s, d in rows_out)
    return pl.pallas_call(
        kernel,
        name=name,
        grid=(steps,),
        in_specs=[SMEM_SPEC] * len(scalars)
        + [row_spec(step_rows, a.shape) for a in rows_in]
        + [whole_spec(a.shape) for a in whole_in]
        + [ANY_SPEC] * len(flat),
        out_specs=[row_spec(step_rows, s) for s, _ in rows_out] + [whole_spec(s) for s, _ in whole_out],
        out_shape=out_shape,
        scratch_shapes=[pltpu.VMEM((width, w_cols), BF), pltpu.SemaphoreType.DMA((n_copies,)), *extra],
        compiler_params=pltpu.CompilerParams(
            dimension_semantics=("arbitrary",), vmem_limit_bytes=VMEM_LIMIT
        ),
        cost_estimate=pl.CostEstimate(flops=flops, bytes_accessed=moved, transcendentals=0),
    )(*scalars, *rows_in, *whole_in, *flat)


class Links:
    def __init__(self, n_dp, n_t, width):
        self.n_dp, self.n_t = n_dp, n_t
        self.rows = width // n_dp
        self.fast = n_dp % 4 == 0 and n_dp & (n_dp - 1) == 0 and self.rows % ROW_TILE == 0
        self.d = lax.axis_index("dp")
        self.t = lax.axis_index("tensor")
        self.nz = n_dp // 4
        self.x, self.y, self.z = self.d % 2, (self.d // 2) % 2, self.d // 4
        n = n_dp * n_t

        def joint(move):
            return [(i, move(i // n_t, i % n_t)) for i in range(n)]

        self.first = joint(lambda d, t: (d ^ (1 if t == 0 else 2)) * n_t + t)
        self.second = joint(lambda d, t: (d ^ (2 if t == 0 else 1)) * n_t + t)
        self.shift = [
            [(i, (i + 4 * j) % n_dp) for i in range(n_dp)] for j in range(self.nz)
        ]
        self.bits = [
            [(i, i ^ (1 << b)) for i in range(n)] for b in range((n - 1).bit_length())
        ]
        self.swap = [(i, i ^ 1) for i in range(n_t)]

    def partner(self, a):
        return lax.ppermute(a, "tensor", self.swap)

    def step(self, a, perm):
        return lax.ppermute(a, ("dp", "tensor"), perm)

    def gather(self, p):
        if not self.fast:
            own = lax.all_gather(p, "dp", axis=0, tiled=True)[None]
            return (own,), (self.partner(own),)
        a = jnp.stack([p] + [lax.ppermute(p, "dp", s) for s in self.shift[1:]])
        a = jnp.concatenate([a, self.step(a, self.first)])
        b = self.step(a, self.second)
        return (a, b), (self.partner(a), self.partner(b))

    def table(self):
        if not self.fast:
            return jnp.zeros((2,), jnp.int32)
        h, s3, s2, j = (
            v.reshape(-1) for v in jnp.meshgrid(*(jnp.arange(k) for k in (2, 2, 2, self.nz)), indexing="ij")
        )
        zero = (self.t ^ h) == 0
        x = self.x ^ jnp.where(zero, s2, s3)
        y = self.y ^ jnp.where(zero, s3, s2)
        z = (self.z - j + self.nz) % self.nz
        return ((z * 2 + y) * 2 + x).astype(jnp.int32)

    def scatter(self, g):
        if not self.fast:
            return lax.psum_scatter(g.astype(F32), "dp", scatter_dimension=0, tiled=True)
        v = g.reshape(self.nz, 2, 2, self.rows, g.shape[1])

        def pick(a, axis, at):
            return lax.dynamic_index_in_dim(a, at, axis, keepdims=False)

        zero = self.t == 0
        send = jnp.where(zero, pick(v, 1, 1 - self.y), pick(v, 2, 1 - self.x))
        held = jnp.where(zero, pick(v, 1, self.y), pick(v, 2, self.x))
        got = self.step(send, self.second)
        held = (held.astype(F32) + got.astype(F32)).astype(BF)
        mine = jnp.where(zero, self.x, self.y)
        got = self.step(pick(held, 1, 1 - mine), self.first)
        held = (pick(held, 1, mine).astype(F32) + got.astype(F32)).astype(BF)
        total = pick(held, 0, self.z).astype(F32)
        for j in range(1, self.nz):
            out = pick(held, 0, (self.z + j) % self.nz)
            total = total + lax.ppermute(out, "dp", self.shift[j]).astype(F32)
        return total

    def total(self, a):
        if not self.fast:
            return lax.psum(a, ("dp", "tensor"))
        for perm in self.bits:
            a = a + self.step(a, perm)
        return a


def weight_grad(links, a, b):
    away = links.partner(tn(a, b[1]).astype(BF))
    return (tn(a, b[0]) + away.astype(F32)).astype(BF)


def per_device(n_dp, n_t, *args):
    (
        images,
        live_images,
        ln1_gain,
        ln1_bias,
        qkv_weight,
        qkv_bias,
        proj_weight,
        proj_bias,
        ln2_gain,
        ln2_bias,
        fc1_weight,
        fc1_bias,
        fc2_weight,
        fc2_bias,
        cotangent,
    ) = args
    micro, slots, seq, _ = images.shape
    width = proj_weight.shape[1] * n_dp
    group = proj_weight.shape[0]
    ff = fc1_weight.shape[1]
    links = Links(n_dp, n_t, width)
    t, rows = links.t, links.rows
    count = micro * slots // n_t
    tall = -(-seq // ROW_TILE) * ROW_TILE
    total_rows = count * tall
    steps = count // BATCH
    step_rows = BATCH * tall

    qkv_shard = qkv_weight.reshape(rows, 3 * group)
    rest_shard = jnp.concatenate([proj_weight.T, fc1_weight, fc2_weight.T], axis=1)
    vectors = [ln1_gain, ln1_bias, proj_bias, ln2_gain, ln2_bias, fc2_bias]
    own_small = jnp.concatenate(vectors + [qkv_bias.reshape(-1), fc1_bias]).astype(F32)
    n_small = own_small.shape[0]
    board = jnp.zeros((n_dp * n_t, n_small), F32)
    board = lax.dynamic_update_slice(board, own_small[None], (links.d * n_t + t, 0))
    board = links.total(board).reshape(n_dp, n_t, n_small)
    qkv_src = links.gather(qkv_shard)
    rest_src = links.gather(rest_shard)
    table = links.table()

    n_vec = len(vectors) * rows
    six = board[:, 0, :n_vec].reshape(n_dp, len(vectors), rows).transpose(1, 0, 2)
    six = six.reshape(len(vectors), width)

    def own_first(a):
        return jnp.where(t == 0, a, a[::-1])

    qb = board[:, :, n_vec : n_vec + qkv_bias.size].reshape(n_dp, n_t, 2, qkv_bias.shape[1])
    qb = qb.transpose(1, 2, 0, 3).reshape(n_t, 2, group)
    qb = jnp.stack([qb[:, 0], jnp.zeros_like(qb[:, 0]), qb[:, 1]], axis=1)
    qb = own_first(qb.reshape(n_t, 3 * group)).reshape(1, -1)
    fb = board[:, :, n_vec + qkv_bias.size :].transpose(1, 0, 2).reshape(n_t, ff)
    fb = own_first(fb).reshape(1, -1)

    def wide(a):
        return jnp.pad(a, ((0, 0), (0, n_t * ff - a.shape[1])))

    vec = jnp.concatenate([wide(six), fb, wide(qb)])

    def mine(a):
        a = a.reshape(micro * slots, seq, width)
        return lax.dynamic_slice_in_dim(a, t * count, count, 0)

    def padded(a):
        return jnp.pad(a, ((0, 0), (0, tall - seq), (0, 0))).reshape(total_rows, width)

    alive = (jnp.arange(slots)[None, :] < live_images).astype(jnp.int32).reshape(-1)
    live = lax.dynamic_slice_in_dim(alive, t * count, count, 0)
    x = padded(mine(images))
    go = padded(mine(cotangent) * live[:, None, None].astype(BF))

    per_half = len(qkv_src[0])
    base = 2 * total_rows * width
    call = functools.partial(run, steps=steps, step_rows=step_rows)
    normed1, qkv, lse, ctx = call(
        functools.partial(attn_fwd_kernel, seq, per_half),
        "attn_fwd",
        scalars=[table],
        rows_in=[x],
        whole_in=[vec],
        sources=qkv_src,
        rows_out=[
            ((total_rows, width), BF),
            ((2, total_rows, 3 * group), BF),
            ((2, total_rows, LANES), F32),
            ((2, total_rows, group), BF),
        ],
        whole_out=[],
        w_cols=6 * group,
        flops=base * 8 * group,
    )
    rest_cols = 2 * rest_shard.shape[1]
    resid, normed2, hidden, slope, act = call(
        functools.partial(mlp_fwd_kernel, per_half),
        "mlp_fwd",
        scalars=[table, live],
        rows_in=[ctx, x],
        whole_in=[vec],
        sources=rest_src,
        rows_out=[
            ((total_rows, width), F32),
            ((total_rows, width), BF),
            ((2, total_rows, ff), BF),
            ((2, total_rows, ff), BF),
            ((total_rows, width), BF),
        ],
        whole_out=[],
        w_cols=rest_cols,
        flops=base * (2 * group + 4 * ff),
        extra=[pltpu.VMEM((step_rows, width), F32)],
    )
    act = act.reshape(count, tall, width)[:, :seq]
    act_away = links.partner(act)
    fc2_sum = links.scatter(weight_grad(links, go, hidden))
    gpre, gr, grb, gctx, small2, fc1b = call(
        functools.partial(mlp_bwd_kernel, per_half),
        "mlp_bwd",
        scalars=[table],
        rows_in=[go, slope, resid],
        whole_in=[vec],
        sources=rest_src,
        rows_out=[
            ((2, total_rows, ff), BF),
            ((total_rows, width), F32),
            ((total_rows, width), BF),
            ((2, total_rows, group), BF),
        ],
        whole_out=[((32, width), F32), ((8, 2 * ff), F32)],
        w_cols=rest_cols,
        flops=base * (2 * group + 4 * ff),
    )
    away = jnp.concatenate([tn(normed2, gpre[1]), tn(grb, ctx[1])], axis=1).astype(BF)
    away = links.partner(away).astype(F32)
    here = jnp.concatenate([tn(normed2, gpre[0]), tn(grb, ctx[0])], axis=1)
    mid_sum = links.scatter((here + away).astype(BF))
    gqkv, gin, small1, qkvb = call(
        functools.partial(attn_bwd_kernel, seq, per_half),
        "attn_bwd",
        scalars=[table],
        rows_in=[qkv, lse, gctx, x, gr],
        whole_in=[vec],
        sources=qkv_src,
        rows_out=[((2, total_rows, 3 * group), BF), ((total_rows, width), BF)],
        whole_out=[((16, width), F32), ((2, 16, group), F32)],
        w_cols=6 * group,
        flops=base * 8 * group,
    )
    gin = gin.reshape(count, tall, width)[:, :seq]
    gin_away = links.partner(gin)
    qkv_sum = links.scatter(weight_grad(links, normed1, gqkv))

    six_grads = jnp.sum(
        jnp.concatenate([small1.reshape(2, 8, width), small2.reshape(4, 8, width)]), axis=1
    )
    qb_grad = own_first(jnp.sum(qkvb.reshape(2, 2, 8, group), axis=2))
    fb_grad = own_first(jnp.sum(fc1b.reshape(8, 2, ff), axis=0))
    flat = jnp.concatenate([six_grads.reshape(-1), qb_grad.reshape(-1), fb_grad.reshape(-1)])
    flat = links.total(flat.reshape(-1, LANES)).reshape(-1)
    n_six = six_grads.size
    six_own = lax.dynamic_slice_in_dim(flat[:n_six].reshape(-1, width), links.d * rows, rows, 1)
    qb_all = flat[n_six : n_six + qb_grad.size].reshape(n_t, 2, n_dp, group // n_dp)
    qb_own = qb_all[t, :, links.d]
    fb_own = flat[n_six + qb_grad.size :].reshape(n_t, n_dp, ff // n_dp)[t, links.d]

    def joined(own, away):
        both = jnp.stack([jnp.where(t == 0, own, away), jnp.where(t == 0, away, own)])
        return both.reshape(micro, slots, seq, width)

    return (
        joined(act, act_away),
        joined(gin, gin_away).astype(F32),
        six_own[0],
        six_own[1],
        qkv_sum.reshape(rows, 3, group),
        qb_own,
        mid_sum[:, ff:].T,
        six_own[4],
        six_own[2],
        six_own[3],
        mid_sum[:, :ff],
        fb_own,
        fc2_sum.T,
        six_own[5],
    )


def solution(mesh):
    in_specs = (
        P(None, "dp", None, None),
        P(None, "dp"),
        P("dp"),
        P("dp"),
        P("dp", None, "tensor"),
        P(None, ("tensor", "dp")),
        P("tensor", "dp"),
        P("dp"),
        P("dp"),
        P("dp"),
        P("dp", "tensor"),
        P(("tensor", "dp")),
        P("tensor", "dp"),
        P("dp"),
        P(None, "dp", None, None),
    )
    out_specs = (
        P(None, "dp", None, None),
        P(None, "dp", None, None),
        P("dp"),
        P("dp"),
        P("dp", None, "tensor"),
        P(None, ("tensor", "dp")),
        P("tensor", "dp"),
        P("dp"),
        P("dp"),
        P("dp"),
        P("dp", "tensor"),
        P(("tensor", "dp")),
        P("tensor", "dp"),
        P("dp"),
    )
    body = functools.partial(per_device, mesh.shape["dp"], mesh.shape["tensor"])
    return jax.shard_map(body, mesh=mesh, in_specs=in_specs, out_specs=out_specs, check_vma=False)
```

time: 1320 us -> 446 us (0.34)
  waiting for transfers between devices: 438 us -> 111 us
  blocking collectives: 234 us -> 0 us
  matrix products: 242 us -> 39.6 us
  other arithmetic: 197 us -> 30.2 us
  Pallas kernels: 0 us -> 147 us
  local copies, waits for them, and re-layouts: 175 us -> 50.2 us
  starting transfers between devices: 0.81 us -> 61.7 us
  between operations: 19 us -> 1.91 us
    reduce_scatter x4 -> x0, waiting for transfers between devices: 388 us -> none  [the longest x1 143 us: per_device(): lax.psum_scatter(totals[10], 'dp', scatter_dimension=1, tiled=True)]
    dot_general x36 -> x8, matrix products: 242 us -> 39.6 us  [tn(): lax.dot_general(a, b, (((0,), (0,)), ((), ())), preferred_element_type=F32)]
    unnamed x2 -> x0, blocking collectives: 157 us -> none
    pallas_call x0 -> x4, Pallas kernels: none -> 147 us  [run(): pl.pallas_call(kernel, name=name, grid=(steps,), in_specs=[SMEM_SPEC] * l...]
    reduce_sum x13 -> x3, other arithmetic: 134 us -> 1.69 us  [the longest x1 0.84 us: per_device(): jnp.sum(jnp.concatenate([small1.reshape(2, 8, width), small2.reshape(4, 8...]
    ppermute x0 -> x44, waiting for transfers between devices: none -> 111 us  [the longest x20 75.9 us: step(): return lax.ppermute(a, ('dp', 'tensor'), perm)]
    another operation x33 -> x3, local copies, waits for them, and re-layouts: 88 us -> 0.24 us  [the longest x1 0.09 us: gather(): a = jnp.stack([p] + [lax.ppermute(p, 'dp', s) for s in self.shift[1:]])]
    all_gather x2 -> x0, blocking collectives: 76.9 us -> none  [the longest x1 41.4 us: per_device(): lax.all_gather(proj_weight, 'dp', axis=1, tiled=True)]
  transfers between devices with their start and end apart: 10 -> 44, of which waited for: 6 -> 15; matrix products, arithmetic and copies ran while one was open for 26% -> 24% of each run, Pallas kernels for 0% -> 6%
where the time goes in v1:
time: 446 us; the launch traced here: 441 us
  Pallas kernels  147 us (33%)
  waiting for transfers between devices  111 us (25%)
  starting transfers between devices  61.7 us (14%)
  local copies, waits for them, and re-layouts  50.2 us (11%)
  matrix products  39.6 us (9%)
  other arithmetic  30.2 us (7%)
    pallas_call x4, Pallas kernels, run(): pl.pallas_call(kernel, name=name, grid=(steps,), in_specs=[SMEM_SPEC] * l...  147 us
    ppermute x20, waiting for transfers between devices, step(): return lax.ppermute(a, ('dp', 'tensor'), perm)  75.9 us
    dot_general x8, matrix products, tn(): lax.dot_general(a, b, (((0,), (0,)), ((), ())), preferred_element_type=F32)  39.6 us
    ppermute x20, starting transfers between devices, step(): return lax.ppermute(a, ('dp', 'tensor'), perm)  32.3 us
    unnamed x70, local copies, waits for them, and re-layouts  31.2 us
    ppermute x6, waiting for transfers between devices, gather(): a = jnp.stack([p] + [lax.ppermute(p, 'dp', s) for s in self.shift[1:]])  20 us
    ppermute x9, waiting for transfers between devices, scatter(): total = total + lax.ppermute(out, 'dp', self.shift[j]).astype(F32)  13.3 us
    ppermute x9, starting transfers between devices, scatter(): total = total + lax.ppermute(out, 'dp', self.shift[j]).astype(F32)  12.8 us
  transfers between devices with their start and end apart: 44, of which 15 were waited for; matrix products, arithmetic and copies ran while one was open for 24% of the time, Pallas kernels for 6%

profile of v1, /device:TPU:0, one launch (start us, length us, event | category | flops | bytes accessed | tf_op | source)
XLA Modules:
  0.0 440.7 jit_solution(14703573974946277228)
XLA Ops:
  16.1 5.0 %collective-permute-done.12 = bf16[48,3456]{1,0:T(8,128)(2,1)S(1)} collective-permute-done((bf16[48,3456]{1,0:T(8,128)(2,1)S(1)}, bf16[48,3456]{1,0:T(8,128)(2,1)S(1)}, u32[]{:S(2)}, u32[]{:S(2)}) %collective-permute-start.12) | collective-permute-done | bytes 331808 | tf_op jit(solution)/shard_map/ppermute | solution.py:397
  21.1 15.0 %collective-permute-done.13 = bf16[48,3456]{1,0:T(8,128)(2,1)S(1)} collective-permute-done((bf16[48,3456]{1,0:T(8,128)(2,1)S(1)}, bf16[48,3456]{1,0:T(8,128)(2,1)S(1)}, u32[]{:S(2)}, u32[]{:S(2)}) %collective-permute-start.13) | collective-permute-done | bytes 331808 | tf_op jit(solution)/shard_map/ppermute | solution.py:397
  40.2 14.0 %collective-permute-done.15 = bf16[4,48,3456]{2,1,0:T(8,128)(2,1)S(1)} collective-permute-done((bf16[4,48,3456]{2,1,0:T(8,128)(2,1)S(1)}, bf16[4,48,3456]{2,1,0:T(8,128)(2,1)S(1)}, u32[]{:S(2)}, u32[]{:S(2)}) %collective-permute-start.15) | collective-permute-done | bytes 1327136 | tf_op jit(solution)/shard_map/ppermute | solution.py:391
  57.5 4.5 %copy.45 = bf16[2,6,197,768]{3,2,1,0:T(8,128)(2,1)} copy(bf16[2,6,197,768]{3,0,2,1:T(2,128)(2,1)} %param.15) | data formatting | bytes 7262208 | tf_op args[0]
  77.0 11.3 %collective-permute-done.2 = f32[32,432]{1,0:T(8,128)S(1)} collective-permute-done((f32[32,432]{1,0:T(8,128)S(1)}, f32[32,432]{1,0:T(8,128)S(1)}, u32[]{:S(2)}, u32[]{:S(2)}) %collective-permute-start.2) | collective-permute-done | bytes 55328 | tf_op jit(solution)/shard_map/ppermute | solution.py:391
  88.3 8.2 %collective-permute-start.3 = (f32[32,432]{1,0:T(8,128)S(1)}, f32[32,432]{1,0:T(8,128)S(1)}, u32[]{:S(2)}, u32[]{:S(2)}) collective-permute-start(f32[32,432]{1,0:T(8,128)S(1)} %add.256), channel_id=1, source_target_pairs={{0,8},{1,9},{2,10},{3,11},{4,12},{5,13},{6,14},{7,15},{8,0},{9,1},... | collective-permute-start | bytes 165896 | tf_op jit(solution)/shard_map/ppermute | solution.py:391
  104.6 5.7 %collective-permute-start.17 = (bf16[8,48,3456]{2,1,0:T(8,128)(2,1)}, bf16[8,48,3456]{2,1,0:T(8,128)(2,1)}, u32[]{:S(2)}, u32[]{:S(2)}) collective-permute-start(bf16[8,48,3456]{2,1,0:T(8,128)(2,1)} %constant_dynamic-update-slice_fusion.5.refs_0_), channel_id=1, source_target_pairs={{0,1},{1,0},{2,3},{3,2},{4,5},{5,4},{6,7},{7,6},{8,9},{9,8},{10,11... | collective-permute-start | bytes 7962632 | tf_op jit(solution)/shard_map/ppermute | solution.py:388
  113.7 10.8 %collective-permute-done.9.refs_1_ = bf16[8,48,1152]{2,1,0:T(8,128)(2,1)S(1)} collective-permute-done((bf16[8,48,1152]{2,1,0:T(8,128)(2,1)}, bf16[8,48,1152]{2,1,0:T(8,128)(2,1)S(1)}, u32[]{:S(2)}, u32[]{:S(2)}) %collective-permute-start.9) | collective-permute-done | bytes 884768 | tf_op jit(solution)/shard_map/ppermute | solution.py:391
  127.0 26.6 %attn_fwd.1 = (bf16[1248,768]{1,0:T(8,128)(2,1)}, bf16[2,1248,1152]{2,1,0:T(8,128)(2,1)}, f32[2,1248,128]{2,1,0:T(8,128)}, bf16[2,1248,384]{2,1,0:T(8,128)(2,1)}) custom-call(s32[32]{0:T(128)} %multiply_add_fusion.table, bf16[1248,768]{1,0:T(8,128)(2,1)} %bitcast.226, f32[8,3072]{1,0:T(8,128)} %select_maximum_fusion.vec_ref, ...), custom_call_target="tpu_custom_call" | custom-call | flops 5888802816 | bytes 16318464 | tf_op jit(solution)/shard_map/attn_fwd/pallas_call | solution.py:345
  153.7 43.2 %mlp_fwd.1 = (f32[1248,768]{1,0:T(8,128)}, bf16[1248,768]{1,0:T(8,128)(2,1)}, bf16[2,1248,1536]{2,1,0:T(8,128)(2,1)}, bf16[2,1248,1536]{2,1,0:T(8,128)(2,1)}, bf16[1248,768]{1,0:T(8,128)(2,1)}) custom-call(s32[32]{0:T(128)} %multiply_add_fusion.table, s32[6]{0:T(128)} %get-tuple-element.81.live, bf16[2,1248,384]{2,1,0:T(8,128)(2,1)} %get-tuple-element.33.ctx_ref, ...), custom_call_target="tpu_custom_call" | custom-call | flops 13249806336 | bytes 37453824 | tf_op jit(solution)/shard_map/mlp_fwd/pallas_call | solution.py:345
  196.9 30.2 %mlp_bwd.1 = (bf16[2,1248,1536]{2,1,0:T(8,128)(2,1)}, f32[1248,768]{1,0:T(8,128)}, bf16[1248,768]{1,0:T(8,128)(2,1)}, bf16[2,1248,384]{2,1,0:T(8,128)(2,1)}, f32[32,768]{1,0:T(8,128)}, /*index=5*/f32[8,3072]{1,0:T(8,128)}) custom-call(s32[32]{0:T(128)} %multiply_add_fusion.table, bf16[1248,768]{1,0:T(8,128)(2,1)} %bitcast.223, ...), custom_call_target="tpu_custom_call" | custom-call | flops 13249806336 | bytes 39370752 | tf_op jit(solution)/shard_map/mlp_bwd/pallas_call | solution.py:345
  227.1 6.1 %fusion.13 = bf16[768,1536]{1,0:T(8,128)(2,1)S(1)} fusion(bf16[1248,768]{1,0:T(8,128)(2,1)} %get-tuple-element.48, bf16[2,1248,1536]{2,1,0:T(8,128)(2,1)} %get-tuple-element.49), kind=kOutput, calls=%fused_computation.19 | convolution fusion | flops 2945581056 | bytes 8110080 | tf_op jit(solution)/shard_map/dot_general | solution.py:53
  233.2 5.0 %fusion.7 = f32[768,1536]{1,0:T(8,128)} fusion(bf16[1248,768]{1,0:T(8,128)(2,1)S(1)} %copy-done.22, bf16[2,1248,1536]{2,1,0:T(8,128)(2,1)S(1)} %copy-done.21), kind=kOutput, calls=%fused_computation.10 | convolution fusion | flops 2944401408 | bytes 10469376 | tf_op jit(solution)/shard_map/dot_general | solution.py:53
  238.2 46.6 %attn_bwd.1 = (bf16[2,1248,1152]{2,1,0:T(8,128)(2,1)}, bf16[1248,768]{1,0:T(8,128)(2,1)}, f32[16,768]{1,0:T(8,128)}, f32[2,16,384]{2,1,0:T(8,128)}) custom-call(s32[32]{0:T(128)} %multiply_add_fusion.table, bf16[2,1248,1152]{2,1,0:T(8,128)(2,1)} %get-tuple-element.35.qkv_ref, f32[2,1248,128]{2,1,0:T(8,128)} %get-tuple-element.36.lse_ref, ...), custom_call_target="tpu_custom_call" | custom-call | flops 5888802816 | bytes 25903104 | tf_op jit(solution)/shard_map/attn_bwd/pallas_call | solution.py:345
  287.2 6.5 %convolution_convert_fusion = bf16[768,1152]{1,0:T(8,128)(2,1)} fusion(bf16[1248,768]{1,0:T(8,128)(2,1)} %get-tuple-element.46, bf16[2,1248,1152]{2,1,0:T(8,128)(2,1)} %get-tuple-element.47), kind=kOutput, calls=%fused_computation.18 | convolution fusion | flops 2209185792 | bytes 6561792 | tf_op jit(solution)/shard_map/dot_general | solution.py:53
  295.6 6.9 %fusion.16 = bf16[768,1536]{1,0:T(8,128)(2,1)} fusion(bf16[1248,768]{1,0:T(8,128)(2,1)S(1)} %bitcast.224, bf16[2,1248,1536]{2,1,0:T(8,128)(2,1)} %get-tuple-element.51), kind=kOutput, calls=%fused_computation.20 | convolution fusion | flops 2945581056 | bytes 8110080 | tf_op jit(solution)/shard_map/dot_general | solution.py:53
  321.0 5.7 %fusion.19 = bf16[768,1152]{1,0:T(8,128)(2,1)S(1)} fusion(bf16[768,1152]{1,0:T(8,128)(2,1)} %collective-permute-done.26, bf16[1248,768]{1,0:T(8,128)(2,1)} %get-tuple-element.46, bf16[2,1248,1152]{2,1,0:T(8,128)(2,1)} %get-tuple-element.47), kind=kOutput, calls=%fused_computation.21 | convolution fusion | flops 2210955264 | bytes 8331264 | tf_op jit(solution)/shard_map/dot_general | solution.py:53
  339.6 12.0 %copy.68 = f32[2,6,197,768]{3,0,2,1:T(2,128)} copy(f32[2,6,197,768]{3,2,1,0:T(8,128)} %maximum_convert_fusion) | data formatting | bytes 14524416
  351.6 6.8 %copy.67 = bf16[2,6,197,768]{3,0,2,1:T(2,128)(2,1)} copy(bf16[2,6,197,768]{3,2,1,0:T(8,128)(2,1)} %pad_maximum_fusion) | data formatting | bytes 7262208
  358.4 5.9 %add_convert_fusion = bf16[768,1536]{1,0:T(8,128)(2,1)S(1)} fusion(bf16[768,1536]{1,0:T(8,128)(2,1)} %collective-permute-done.38, bf16[1248,768]{1,0:T(8,128)(2,1)S(1)} %bitcast.225, bf16[2,1248,1536]{2,1,0:T(8,128)(2,1)} %get-tuple-element.51), kind=kOutput, calls=%fused_computation.2 | convolution fusion | flops 2947940352 | bytes 10469376 | tf_op jit(solution)/shard_map/dot_general | solution.py:53
  372.7 8.2 %collective-permute-done.28 = bf16[4,48,1152]{2,1,0:T(8,128)(2,1)S(1)} collective-permute-done((bf16[4,48,1152]{2,1,0:T(8,128)(2,1)S(1)}, bf16[4,48,1152]{2,1,0:T(8,128)(2,1)S(1)}, u32[]{:S(2)}, u32[]{:S(2)}) %collective-permute-start.28) | collective-permute-done | bytes 442400 | tf_op jit(solution)/shard_map/ppermute | solution.py:391
  387.0 21.0 %collective-permute-done.33 = bf16[4,2,48,1920]{3,2,0,1:T(8,128)(2,1)S(1)} collective-permute-done((bf16[4,2,48,1920]{3,2,0,1:T(8,128)(2,1)S(1)}, bf16[4,2,48,1920]{3,2,0,1:T(8,128)(2,1)S(1)}, u32[]{:S(2)}, u32[]{:S(2)}) %collective-permute-start.33) | collective-permute-done | bytes 1474592 | tf_op jit(solution)/shard_map/ppermute | solution.py:391
  414.5 5.7 %collective-permute-done.34 = bf16[4,48,1920]{2,1,0:T(8,128)(2,1)S(1)} collective-permute-done((bf16[4,48,1920]{2,1,0:T(8,128)(2,1)S(1)}, bf16[4,48,1920]{2,1,0:T(8,128)(2,1)S(1)}, u32[]{:S(2)}, u32[]{:S(2)}) %collective-permute-start.34) | collective-permute-done | bytes 737312 | tf_op jit(solution)/shard_map/ppermute | solution.py:391
  429.7 9.0 %collective-permute-done.36 = bf16[48,1920]{1,0:T(8,128)(2,1)S(1)} collective-permute-done((bf16[48,1920]{1,0:T(8,128)(2,1)S(1)}, bf16[48,1920]{1,0:T(8,128)(2,1)S(1)}, u32[]{:S(2)}, u32[]{:S(2)}) %collective-permute-start.36) | collective-permute-done | bytes 184352 | tf_op jit(solution)/shard_map/ppermute | solution.py:433
  (259 shorter events, 118.9 us)
Async XLA Ops:
  1.7 73.9 %collective-permute-start.5 = (bf16[48,1152]{1,0:T(8,128)(2,1)S(1)}, bf16[48,1152]{1,0:T(8,128)(2,1)S(1)}, u32[]{:S(2)}, u32[]{:S(2)}) collective-permute-start(bf16[48,1152]{1,0:T(8,128)(2,1)S(1)} %bitcast.244), channel_id=1, source_target_pairs={{0,8},{2,10},{4,12},{6,14},{8,16},{10,18},{12,20},{14,22},{16,24},... | collective-permute-start | bytes 331784 | tf_op jit(solution)/shard_map/ppermute | solution.py:397
  4.8 70.8 %collective-permute-start.6 = (bf16[48,1152]{1,0:T(8,128)(2,1)S(1)}, bf16[48,1152]{1,0:T(8,128)(2,1)S(1)}, u32[]{:S(2)}, u32[]{:S(2)}) collective-permute-start(bf16[48,1152]{1,0:T(8,128)(2,1)S(1)} %bitcast.245), channel_id=1, source_target_pairs={{0,16},{2,18},{4,20},{6,22},{8,24},{10,26},{12,28},{14,30},{16,0},... | collective-permute-start | bytes 331784 | tf_op jit(solution)/shard_map/ppermute | solution.py:397
  8.6 27.5 %collective-permute-start.13 = (bf16[48,3456]{1,0:T(8,128)(2,1)S(1)}, bf16[48,3456]{1,0:T(8,128)(2,1)S(1)}, u32[]{:S(2)}, u32[]{:S(2)}) collective-permute-start(bf16[48,3456]{1,0:T(8,128)(2,1)S(1)} %get-tuple-element.108), channel_id=1, source_target_pairs={{0,16},{2,18},{4,20},{6,22},{8,24},{10,26},{12,28},{14,30},{16,0},... | collective-permute-start | bytes 995336 | tf_op jit(solution)/shard_map/ppermute | solution.py:397
  10.4 25.7 %collective-permute-start.14 = (bf16[48,3456]{1,0:T(8,128)(2,1)S(1)}, bf16[48,3456]{1,0:T(8,128)(2,1)S(1)}, u32[]{:S(2)}, u32[]{:S(2)}) collective-permute-start(bf16[48,3456]{1,0:T(8,128)(2,1)S(1)} %get-tuple-element.108), channel_id=1, source_target_pairs={{0,24},{2,26},{4,28},{6,30},{8,0},{10,2},{12,4},{14,6},{16,8},{18,... | collective-permute-start | bytes 995336 | tf_op jit(solution)/shard_map/ppermute | solution.py:397
  21.1 54.6 %collective-permute-start.7 = (bf16[48,1152]{1,0:T(8,128)(2,1)S(1)}, bf16[48,1152]{1,0:T(8,128)(2,1)S(1)}, u32[]{:S(2)}, u32[]{:S(2)}) collective-permute-start(bf16[48,1152]{1,0:T(8,128)(2,1)S(1)} %bitcast.246), channel_id=1, source_target_pairs={{0,24},{2,26},{4,28},{6,30},{8,0},{10,2},{12,4},{14,6},{16,8},{18,... | collective-permute-start | bytes 331784 | tf_op jit(solution)/shard_map/ppermute | solution.py:397
  36.1 32.0 %collective-permute-start = (f32[32,432]{1,0:T(8,128)S(1)}, f32[32,432]{1,0:T(8,128)S(1)}, u32[]{:S(2)}, u32[]{:S(2)}) collective-permute-start(f32[32,432]{1,0:T(8,128)S(1)} %dynamic_update_slice.5), channel_id=1, source_target_pairs={{0,1},{1,0},{2,3},{3,2},{4,5},{5,4},{6,7},{7,6},{8,9},{9,8},{10,11... | collective-permute-start | bytes 165896 | tf_op jit(solution)/shard_map/ppermute | solution.py:391
  36.3 17.8 %collective-permute-start.15 = (bf16[4,48,3456]{2,1,0:T(8,128)(2,1)S(1)}, bf16[4,48,3456]{2,1,0:T(8,128)(2,1)S(1)}, u32[]{:S(2)}, u32[]{:S(2)}) collective-permute-start(bf16[4,48,3456]{2,1,0:T(8,128)(2,1)S(1)} %pad_maximum_fusion.2), channel_id=1, source_target_pairs={{0,2},{1,5},{2,0},{3,7},{4,6},{5,1},{6,4},{7,3},{8,10},{9,13},{10,... | collective-permute-start | bytes 3981320 | tf_op jit(solution)/shard_map/ppermute | solution.py:391
  55.4 55.0 %collective-permute-start.16 = (bf16[8,48,3456]{2,1,0:T(8,128)(2,1)}, bf16[8,48,3456]{2,1,0:T(8,128)(2,1)}, u32[]{:S(2)}, u32[]{:S(2)}) collective-permute-start(bf16[8,48,3456]{2,1,0:T(8,128)(2,1)} %constant_dynamic-update-slice_fusion.5.refs_0_), channel_id=1, source_target_pairs={{0,4},{1,3},{2,6},{3,1},{4,0},{5,7},{6,2},{7,5},{8,12},{9,11},{10,... | collective-permute-start | bytes 7962632 | tf_op jit(solution)/shard_map/ppermute | solution.py:391
  75.8 34.7 %collective-permute-start.8 = (bf16[4,48,1152]{2,1,0:T(8,128)(2,1)S(1)}, bf16[4,48,1152]{2,1,0:T(8,128)(2,1)S(1)}, u32[]{:S(2)}, u32[]{:S(2)}) collective-permute-start(bf16[4,48,1152]{2,1,0:T(8,128)(2,1)S(1)} %pad_maximum_fusion.3), channel_id=1, source_target_pairs={{0,2},{1,5},{2,0},{3,7},{4,6},{5,1},{6,4},{7,3},{8,10},{9,13},{10,... | collective-permute-start | bytes 1327112 | tf_op jit(solution)/shard_map/ppermute | solution.py:391
  104.6 49.1 %collective-permute-start.17 = (bf16[8,48,3456]{2,1,0:T(8,128)(2,1)}, bf16[8,48,3456]{2,1,0:T(8,128)(2,1)}, u32[]{:S(2)}, u32[]{:S(2)}) collective-permute-start(bf16[8,48,3456]{2,1,0:T(8,128)(2,1)} %constant_dynamic-update-slice_fusion.5.refs_0_), channel_id=1, source_target_pairs={{0,1},{1,0},{2,3},{3,2},{4,5},{5,4},{6,7},{7,6},{8,9},{9,8},{10,11... | collective-permute-start | bytes 7962632 | tf_op jit(solution)/shard_map/ppermute | solution.py:388
  110.3 43.4 %collective-permute-start.18 = (bf16[8,48,3456]{2,1,0:T(8,128)(2,1)}, bf16[8,48,3456]{2,1,0:T(8,128)(2,1)}, u32[]{:S(2)}, u32[]{:S(2)}) collective-permute-start(bf16[8,48,3456]{2,1,0:T(8,128)(2,1)} %collective-permute-done.16.refs_1_), channel_id=1, source_target_pairs={{0,1},{1,0},{2,3},{3,2},{4,5},{5,4},{6,7},{7,6},{8,9},{9,8},{10,11... | collective-permute-start | bytes 7962632 | tf_op jit(solution)/shard_map/ppermute | solution.py:388
  293.7 27.4 %collective-permute-start.26 = (bf16[768,1152]{1,0:T(8,128)(2,1)}, bf16[768,1152]{1,0:T(8,128)(2,1)}, u32[]{:S(2)}, u32[]{:S(2)}) collective-permute-start(bf16[768,1152]{1,0:T(8,128)(2,1)} %convolution_convert_fusion), channel_id=1, source_target_pairs={{0,1},{1,0},{2,3},{3,2},{4,5},{5,4},{6,7},{7,6},{8,9},{9,8},{10,11... | collective-permute-start | bytes 5308424 | tf_op jit(solution)/shard_map/ppermute | solution.py:388
  310.6 47.8 %collective-permute-start.38 = (bf16[768,1536]{1,0:T(8,128)(2,1)}, bf16[768,1536]{1,0:T(8,128)(2,1)}, u32[]{:S(2)}, u32[]{:S(2)}) collective-permute-start(bf16[768,1536]{1,0:T(8,128)(2,1)} %fusion.16), channel_id=1, source_target_pairs={{0,1},{1,0},{2,3},{3,2},{4,5},{5,4},{6,7},{7,6},{8,9},{9,8},{10,11... | collective-permute-start | bytes 7077896 | tf_op jit(solution)/shard_map/ppermute | solution.py:388
  315.7 52.7 %collective-permute-start.32 = (bf16[768,1920]{1,0:T(8,128)(2,1)}, bf16[768,1920]{1,0:T(8,128)(2,1)}, u32[]{:S(2)}, u32[]{:S(2)}) collective-permute-start(bf16[768,1920]{1,0:T(8,128)(2,1)} %pad_maximum_fusion.1), channel_id=1, source_target_pairs={{0,1},{1,0},{2,3},{3,2},{4,5},{5,4},{6,7},{7,6},{8,9},{9,8},{10,11... | collective-permute-start | bytes 8847368 | tf_op jit(solution)/shard_map/ppermute | solution.py:388
  319.1 16.7 %collective-permute-start.19 = (bf16[6,197,768]{2,1,0:T(8,128)(2,1)}, bf16[6,197,768]{2,1,0:T(8,128)(2,1)}, u32[]{:S(2)}, u32[]{:S(2)}) collective-permute-start(bf16[6,197,768]{2,1,0:T(8,128)(2,1)} %slice.112), channel_id=1, source_target_pairs={{0,1},{1,0},{2,3},{3,2},{4,5},{5,4},{6,7},{7,6},{8,9},{9,8},{10,11... | collective-permute-start | bytes 5446664 | tf_op jit(solution)/shard_map/ppermute | solution.py:388
  329.0 36.7 %collective-permute-start.27 = (bf16[4,2,48,1152]{3,2,0,1:T(8,128)(2,1)}, bf16[4,2,48,1152]{3,2,0,1:T(8,128)(2,1)}, u32[]{:S(2)}, u32[]{:S(2)}) collective-permute-start(bf16[4,2,48,1152]{3,2,0,1:T(8,128)(2,1)} %bitcast_select_fusion.4), channel_id=1, source_target_pairs={{0,4},{1,3},{2,6},{3,1},{4,0},{5,7},{6,2},{7,5},{8,12},{9,11},{10,... | collective-permute-start | bytes 2654216 | tf_op jit(solution)/shard_map/ppermute | solution.py:391
  364.9 21.0 %collective-permute-start.39 = (bf16[4,2,48,1536]{3,2,0,1:T(8,128)(2,1)S(1)}, bf16[4,2,48,1536]{3,2,0,1:T(8,128)(2,1)S(1)}, u32[]{:S(2)}, u32[]{:S(2)}) collective-permute-start(bf16[4,2,48,1536]{3,2,0,1:T(8,128)(2,1)S(1)} %bitcast_select_fusion.2), channel_id=1, source_target_pairs={{0,4},{1,3},{2,6},{3,1},{4,0},{5,7},{6,2},{7,5},{8,12},{9,11},{10,... | collective-permute-start | bytes 3538952 | tf_op jit(solution)/shard_map/ppermute | solution.py:391
  371.8 36.2 %collective-permute-start.33 = (bf16[4,2,48,1920]{3,2,0,1:T(8,128)(2,1)S(1)}, bf16[4,2,48,1920]{3,2,0,1:T(8,128)(2,1)S(1)}, u32[]{:S(2)}, u32[]{:S(2)}) collective-permute-start(bf16[4,2,48,1920]{3,2,0,1:T(8,128)(2,1)S(1)} %bitcast_select_fusion), channel_id=1, source_target_pairs={{0,4},{1,3},{2,6},{3,1},{4,0},{5,7},{6,2},{7,5},{8,12},{9,11},{10,... | collective-permute-start | bytes 4423688 | tf_op jit(solution)/shard_map/ppermute | solution.py:391
  381.1 28.1 %collective-permute-start.29 = (bf16[48,1152]{1,0:T(8,128)(2,1)S(1)}, bf16[48,1152]{1,0:T(8,128)(2,1)S(1)}, u32[]{:S(2)}, u32[]{:S(2)}) collective-permute-start(bf16[48,1152]{1,0:T(8,128)(2,1)S(1)} %get-tuple-element.104), channel_id=1, source_target_pairs={{0,8},{2,10},{4,12},{6,14},{8,16},{10,18},{12,20},{14,22},{16,24},... | collective-permute-start | bytes 331784 | tf_op jit(solution)/shard_map/ppermute | solution.py:433
  382.9 26.3 %collective-permute-start.30 = (bf16[48,1152]{1,0:T(8,128)(2,1)S(1)}, bf16[48,1152]{1,0:T(8,128)(2,1)S(1)}, u32[]{:S(2)}, u32[]{:S(2)}) collective-permute-start(bf16[48,1152]{1,0:T(8,128)(2,1)S(1)} %get-tuple-element.106), channel_id=1, source_target_pairs={{0,16},{2,18},{4,20},{6,22},{8,24},{10,26},{12,28},{14,30},{16,0},... | collective-permute-start | bytes 331784 | tf_op jit(solution)/shard_map/ppermute | solution.py:433
  383.0 26.2 %collective-permute-start.31 = (bf16[48,1152]{1,0:T(8,128)(2,1)S(1)}, bf16[48,1152]{1,0:T(8,128)(2,1)S(1)}, u32[]{:S(2)}, u32[]{:S(2)}) collective-permute-start(bf16[48,1152]{1,0:T(8,128)(2,1)S(1)} %get-tuple-element.105), channel_id=1, source_target_pairs={{0,24},{2,26},{4,28},{6,30},{8,0},{10,2},{12,4},{14,6},{16,8},{18,... | collective-permute-start | bytes 331784 | tf_op jit(solution)/shard_map/ppermute | solution.py:433
  386.4 23.6 %collective-permute-start.40 = (bf16[4,48,1536]{2,1,0:T(8,128)(2,1)S(1)}, bf16[4,48,1536]{2,1,0:T(8,128)(2,1)S(1)}, u32[]{:S(2)}, u32[]{:S(2)}) collective-permute-start(bf16[4,48,1536]{2,1,0:T(8,128)(2,1)S(1)} %dynamic-slice_bitcast_fusion.1), channel_id=1, source_target_pairs={{0,2},{1,5},{2,0},{3,7},{4,6},{5,1},{6,4},{7,3},{8,10},{9,13},{10,... | collective-permute-start | bytes 1769480 | tf_op jit(solution)/shard_map/ppermute | solution.py:391
  422.2 16.5 %collective-permute-start.36 = (bf16[48,1920]{1,0:T(8,128)(2,1)S(1)}, bf16[48,1920]{1,0:T(8,128)(2,1)S(1)}, u32[]{:S(2)}, u32[]{:S(2)}) collective-permute-start(bf16[48,1920]{1,0:T(8,128)(2,1)S(1)} %get-tuple-element.100), channel_id=1, source_target_pairs={{0,16},{2,18},{4,20},{6,22},{8,24},{10,26},{12,28},{14,30},{16,0},... | collective-permute-start | bytes 552968 | tf_op jit(solution)/shard_map/ppermute | solution.py:433
  422.3 16.5 %collective-permute-start.37 = (bf16[48,1920]{1,0:T(8,128)(2,1)S(1)}, bf16[48,1920]{1,0:T(8,128)(2,1)S(1)}, u32[]{:S(2)}, u32[]{:S(2)}) collective-permute-start(bf16[48,1920]{1,0:T(8,128)(2,1)S(1)} %get-tuple-element.99), channel_id=1, source_target_pairs={{0,24},{2,26},{4,28},{6,30},{8,0},{10,2},{12,4},{14,6},{16,8},{18,... | collective-permute-start | bytes 552968 | tf_op jit(solution)/shard_map/ppermute | solution.py:433
  (47 other events, 489.7 us)
